TPU v7x, 128 devices: a whole 4x4x4 slice. The times are simulated.
128 devices in a mesh: req: 4 (over x), exp: 32 (over z, y, core).
Axes of the slice: x: 4, y: 4, z: 4, core: 2. Of those that a mesh axis runs over, the one named last changes fastest.
Arguments:
- hidden_in: bfloat16 [4, 32, 128, 2048], P('req', 'exp'), may hold values from -6 to 6
- queries: bfloat16 [4, 32, 128, 2048], P('req', 'exp'), may hold values from -6 to 6
- suffix_pairs: bfloat16 [4, 32, 2, 128, 2048], P('req', 'exp'), may hold values from -6 to 6
- prefix_cache: bfloat16 [32, 4, 2, 384, 2048], P('exp', 'req'), may hold values from -6 to 6
- suffix_length: int32 [4, 32], P('req', 'exp'), may hold values from 1 to 128, 3072 in all within a row
- request_group: int32 [4, 32], P('req', 'exp'), may hold values from 0 to 3
- prefix_owner: int32 [32, 4], P('exp'), may hold values from 0 to 3, each once within a row
- out_weight: bfloat16 [2048, 2048], replicated, may hold values from -0.8984375 to 0.8984375
- norm_gain: float32 [2048], replicated, may hold values from 0.1 to 1.9
- routes: int32 [4, 32, 128, 8], P('req', 'exp'), may hold values from 0 to 31, all different within a row; in each aligned block of 128 rows (0 to 127, 128 to 255, ..., all dimensions but the last counted through in order) at most 40 rows name the same one
- gate_values: float32 [4, 32, 128, 8], P('req', 'exp'), may hold values from 0.05 to 0.3
- expert_upward: bfloat16 [32, 2048, 2048], P('exp'), may hold values from -0.125 to 0.125
- expert_downward: bfloat16 [32, 1024, 2048], P('exp'), may hold values from -0.1875 to 0.1875
Outputs:
- layer_out: bfloat16 [4, 32, 128, 2048], P('req', 'exp')
Inputs may be any that keep to these rules, and one draw needn't show every extreme that they name: The request at row r and column e reads the group held at prefix_cache[e, prefix_owner[e, request_group[r, e]]]. `prefix_owner`: each row is a permutation of 0 to 3. `routes`: a row names 8 different experts; on the rows of one device no expert is named more than 40 times, and on the rows of some device one expert is named exactly 40 times.
All inputs are finite; a program needn't handle non-finite values. No bound on the sum of `suffix_length` on one device may be relied on, other than what follows from the above.
Results may differ from a plain program's by a relative error of at most 0.0052.
Values may be sent and summed in bfloat16 or wider, within the bound.
A program may use at most 128 MiB of HBM per device.

v0:
```python
import jax
import jax.numpy as jnp
from jax import lax
from jax.sharding import PartitionSpec as P

HD = 128
SINK = 4


def softmax_part(scores, visible, values):
    masked = jnp.where(visible[None], scores, -jnp.inf)
    largest = jnp.max(masked, axis=2)
    weights = jnp.exp(masked - largest[:, :, None])
    totals = jnp.sum(weights, axis=2)
    summed = jnp.einsum(
        "htc,chd->htd", weights.astype(jnp.bfloat16), values, preferred_element_type=jnp.float32
    )
    return (largest, totals, summed)


def prefix_part(query_heads, cache):
    row_count = query_heads.shape[0]
    head_count = query_heads.shape[1]
    window = cache.shape[1]
    cache_keys = cache[0].reshape(window, head_count, HD)
    cache_values = cache[1].reshape(window, head_count, HD)
    scores = jnp.einsum(
        "thd,chd->htc", query_heads, cache_keys, preferred_element_type=jnp.float32
    ) * HD ** (-0.5)
    column = lax.broadcasted_iota(jnp.int32, (row_count, window), 1)
    position = lax.broadcasted_iota(jnp.int32, (row_count, window), 0)
    return softmax_part(scores, (column < SINK) | (column > position), cache_values)


def suffix_part(query_heads, pairs):
    row_count = query_heads.shape[0]
    head_count = query_heads.shape[1]
    own_keys = pairs[0].reshape(row_count, head_count, HD)
    own_values = pairs[1].reshape(row_count, head_count, HD)
    scores = jnp.einsum(
        "thd,shd->hts", query_heads, own_keys, preferred_element_type=jnp.float32
    ) * HD ** (-0.5)
    column = lax.broadcasted_iota(jnp.int32, (row_count, row_count), 1)
    position = lax.broadcasted_iota(jnp.int32, (row_count, row_count), 0)
    visible = column <= position
    return softmax_part(scores, visible, own_values)


def merge_parts(first, second):
    largest = jnp.maximum(first[0], second[0])
    scale_first = jnp.exp(first[0] - largest)
    scale_second = jnp.exp(second[0] - largest)
    totals = first[1] * scale_first + second[1] * scale_second
    summed = first[2] * scale_first[:, :, None] + second[2] * scale_second[:, :, None]
    merged = summed / totals[:, :, None]
    head_count = merged.shape[0]
    row_count = merged.shape[1]
    return jnp.transpose(merged, (1, 0, 2)).reshape(row_count, head_count * HD).astype(jnp.bfloat16)


def on_device(
    hidden_in,
    queries,
    suffix_pairs,
    prefix_cache,
    suffix_length,
    request_group,
    prefix_owner,
    out_weight,
    norm_gain,
    routes,
    gate_values,
    expert_upward,
    expert_downward,
):
    row_count = hidden_in.shape[2]
    width = hidden_in.shape[3]
    head_count = width // HD
    query_rows = queries[0, 0]
    query_heads = query_rows.reshape(row_count, head_count, HD)
    owner = prefix_owner[0, request_group[0, 0]]
    blank_stats = jnp.zeros((head_count, row_count), jnp.float32)
    blank_sums = jnp.zeros((head_count, row_count, HD), jnp.float32)
    carry = (blank_stats, blank_stats, blank_sums)
    piece = lax.all_gather(prefix_cache, "req", axis=1, tiled=True)
    start = jnp.int32(0)
    held = piece.shape[1]
    inside = (owner >= start) & (owner < start + held)
    offset = jnp.clip(owner, 0, held - 1)

    def attend_piece(ignored):
        cache = lax.dynamic_index_in_dim(piece[0], offset, 0, keepdims=False)
        return prefix_part(query_heads, cache)

    def keep_carry(ignored):
        return carry

    prefix_stats = lax.cond(inside, attend_piece, keep_carry, 0)
    suffix_stats = suffix_part(query_heads, suffix_pairs[0, 0])
    attention = merge_parts(prefix_stats, suffix_stats)
    mixed = jnp.dot(attention, out_weight, preferred_element_type=jnp.float32)
    residual = hidden_in[0, 0].astype(jnp.float32) + mixed
    scaled = residual * lax.rsqrt(jnp.mean(residual * residual, axis=1, keepdims=True) + 1e-05)
    normed = (scaled * norm_gain[None, :]).astype(jnp.bfloat16)
    flat_routes = routes[0, 0].reshape(-1)
    entry_count = flat_routes.shape[0]
    top_count = routes.shape[3]
    column_count = lax.axis_size("exp")
    local_count = expert_downward.shape[0]
    expert_count = local_count * column_count
    capacity = min(row_count, (row_count * top_count * 5 // (4 * expert_count) + 7) // 8 * 8)
    expert_ids = jnp.arange(expert_count, dtype=jnp.int32)
    chosen = (flat_routes[:, None] == expert_ids[None, :]).astype(jnp.int32)
    earlier = jnp.cumsum(chosen, axis=0) - chosen
    slot_rank = jnp.sum(earlier * chosen, axis=1)
    slot_of = flat_routes * capacity + slot_rank
    slot_count = expert_count * capacity
    source = (
        jnp.full((slot_count,), entry_count, jnp.int32)
        .at[slot_of]
        .set(jnp.arange(entry_count, dtype=jnp.int32))
    )
    filled = source < entry_count
    token_of = jnp.minimum(source, entry_count - 1) // top_count
    outgoing_rows = jnp.where(filled[:, None], normed[token_of], jnp.zeros((), jnp.bfloat16))
    outgoing_rows = outgoing_rows.reshape(column_count, local_count, capacity, width)
    joined = jnp.einsum(
        "sekd,edf->sekf",
        lax.all_to_all(outgoing_rows, "exp", split_axis=0, concat_axis=0, tiled=True),
        expert_upward,
        preferred_element_type=jnp.float32,
    )
    inner_width = joined.shape[3] // 2
    hidden_units = (jax.nn.silu(joined[..., :inner_width]) * joined[..., inner_width:]).astype(
        jnp.bfloat16
    )
    produced = jnp.einsum(
        "sekf,efd->sekd", hidden_units, expert_downward, preferred_element_type=jnp.float32
    ).astype(jnp.bfloat16)
    returned_rows = lax.all_to_all(produced, "exp", split_axis=0, concat_axis=0, tiled=True)
    per_entry = returned_rows.reshape(slot_count, width)[slot_of].reshape(
        row_count, top_count, width
    )
    weighted = jnp.sum(per_entry.astype(jnp.float32) * gate_values[0, 0][:, :, None], axis=1)
    combined = residual + weighted
    live_rows = jnp.arange(row_count, dtype=jnp.int32) < suffix_length[0, 0]
    layer_out = jnp.where(live_rows[:, None], combined, 0.0).astype(jnp.bfloat16)
    return layer_out.reshape(1, 1, row_count, width)


def solution(mesh):
    in_specs = (
        P("req", "exp", None, None),
        P("req", "exp", None, None),
        P("req", "exp", None, None, None),
        P("exp", "req", None, None, None),
        P("req", "exp"),
        P("req", "exp"),
        P("exp", None),
        P(),
        P(),
        P("req", "exp", None, None),
        P("req", "exp", None, None),
        P("exp", None, None),
        P("exp", None, None),
    )
    out_specs = P("req", "exp", None, None)
    return jax.shard_map(
        on_device, mesh=mesh, in_specs=in_specs, out_specs=out_specs, check_vma=False
    )
```

profile of v0, /device:TPU:0, one launch (start us, length us, event | category | flops | bytes accessed | tf_op | source)
XLA Modules:
  0.0 357.6 jit_solution(14926072692612265860)
XLA Ops:
  6.5 0.0 all-gather.2.cloned.1.call-start
  6.5 0.7 all-gather.2.cloned.1.call-update
  7.9 0.0 copy-done
  7.9 0.6 constant_dynamic-slice_fusion.2
  9.8 0.8 copy.51
  10.6 0.1 eq.29
  10.7 0.1 eq.25
  10.8 1.3 copy.41
  12.1 0.1 fusion.50
  12.2 0.3 copy.67
  12.5 0.3 copy.48
  12.8 9.0 %reduce-window.6 = s32[32,8,128]{2,1,0:T(8,128)S(1)} reduce-window(s32[32,8,128]{2,1,0:T(8,128)S(1)} %fusion.40, s32[]{:T(128)} %constant.26.clone.1), window={size=1x1x128 pad=0_0x0_0x127_0}, to_apply=%region_6.7 | reduce-window | flops 4161536 | bytes 262148 | tf_op jit(solution)/shard_map/reduce-window
  21.8 0.1 slice.38
  21.9 0.1 copy.53
  22.1 0.1 copy.54
  22.1 0.1 copy.50
  22.2 0.1 mul.99
  22.4 0.1 broadcast_add_fusion
  22.5 4.3 %scatter_custom_fusion = s32[1280]{0:T(1024)S(1)} fusion(s32[1024]{0:T(1024)S(1)} %bitcast.118, s32[1024]{0:T(1024)S(1)} %iota.53, s32[]{:T(128)} %constant.59.clone.1), kind=kCustom, calls=%fused_computation.73 | custom fusion | bytes 5124 | tf_op jit(solution)/shard_map/scatter | solution.py:121
  26.9 0.1 broadcast_in_dim.76
  27.0 0.4 fusion.51
  27.4 0.2 fusion.32
  27.6 102.5 %all-gather.2.cloned.1.call-done = bf16[1,4,2,384,2048]{4,3,2,0,1:T(8,128)(2,1)} async-done(((bf16[1,1,2,384,2048]{4,3,2,0,1:T(8,128)(2,1)}), bf16[1,4,2,384,2048]{4,3,2,0,1:T(8,128)(2,1)}) %all-gather.2.cloned.1.call-update) | async-done | bytes 12582928 | tf_op jit(solution)/shard_map/all_gather | solution.py:85
  130.0 24.1 %conditional.1 = (f32[16,128]{1,0:T(8,128)}, f32[16,128]{1,0:T(8,128)S(1)}, f32[16,128,128]{1,2,0:T(8,128)S(1)}) conditional(s32[]{:T(128)} %convert_element_type.60, () %tuple.13, (s32[]{:T(128)}, bf16[1,4,2,384,2048]{4,3,2,0,1:T(8,128)(2,1)}, bf16[128,16,128]{0,2,1:T(8,128)(2,1)S(1)}) %tuple.30), branch_computations={%region_0.1_spmd, %region_1.4_spmd} | conditional | flops 411398528 | bytes 45843268 | solution.py:98
  130.0 0.1 fusion.9
  130.2 16.7 %copy.42 = bf16[1,4,2,384,2048]{3,4,2,1,0:T(8,128)(2,1)} copy(bf16[1,4,2,384,2048]{4,3,2,0,1:T(8,128)(2,1)} %get-tuple-element.28) | data formatting | bytes 25165824 | tf_op jit(solution)/shard_map
  147.5 2.2 constant_dynamic-slice_fusion.1
  149.7 1.4 fusion.2
  151.1 1.7 fusion.3
  152.8 1.4 fusion.1
  154.2 0.0 copy-start.3
  154.2 0.8 multiply_add_fusion
  155.0 0.4 fusion.31
  155.3 0.0 copy-start.5
  155.3 4.8 %multiply_reduce_fusion = (f32[128]{0:T(128)S(1)}, f32[128,2048]{1,0:T(8,128)S(1)}) fusion(bf16[128,2048]{0,1:T(8,128)(2,1)S(1)} %bitcast.112, bf16[2048,2048]{1,0:T(8,128)(2,1)} %param.22, bf16[1,1,128,2048]{3,2,1,0:T(8,128)(2,1)S(1)} %copy-done.3), kind=kOutput, calls=%fused_computation.42 | convolution fusion | flops 1074790272 | bytes 10486272 | tf_op jit(solution)/shard_map/dot_general | solution.py:101
  160.1 0.2 multiply_convert_fusion
  160.3 6.1 %gather_fusion = bf16[1280,2048]{1,0:T(8,128)(2,1)} fusion(bf16[128,2048]{1,0:T(8,128)(2,1)S(1)} %multiply_convert_fusion, s32[2048]{0:T(1024)S(1)} %pad_clamp_fusion), kind=kCustom, calls=%fused_computation | custom fusion | bytes 10490880 | tf_op jit(solution)/shard_map/gather | solution.py:125
  166.4 2.9 broadcast_select_fusion
  169.3 69.2 %all_to_all.10 = bf16[32,1,40,2048]{3,2,1,0:T(8,128)(2,1)S(1)} all-to-all(bf16[32,1,40,2048]{3,2,1,0:T(8,128)(2,1)S(1)} %broadcast_select_fusion), channel_id=1, replica_groups=mesh['req'=4,'exp'=32] {'exp'}, dimensions={0} | all-to-all | bytes 10485760 | tf_op jit(solution)/shard_map/all_to_all | solution.py:129
  238.6 13.9 %fusion.17 = f32[32,1,40,2048]{3,2,0,1:T(8,128)S(1)} fusion(bf16[1,2048,2048]{2,1,0:T(8,128)(2,1)} %param.26, bf16[32,1,40,2048]{3,2,1,0:T(8,128)(2,1)S(1)} %all_to_all.10), kind=kOutput, calls=%fused_computation.29 | convolution fusion | flops 10737418240 | bytes 24117248 | tf_op jit(solution)/shard_map/sekd,edf->sekf/dot_general | solution.py:127
  252.5 7.8 %convert_bitcast_fusion = bf16[32,1,40,2048]{3,2,1,0:T(8,128)(2,1)} fusion(bf16[1,1024,2048]{2,1,0:T(8,128)(2,1)S(1)} %copy-done.7, f32[32,1,40,2048]{3,2,0,1:T(8,128)S(1)} %fusion.17), kind=kOutput, calls=%fused_computation.27 | convolution fusion | flops 5379194880 | bytes 19922944 | tf_op jit(solution)/shard_map/sekf,efd->sekd/dot_general | solution.py:137
  260.2 5.2 %all-to-all-start.1 = ((bf16[32,1,40,2048]{3,2,1,0:T(8,128)(2,1)}), bf16[32,1,40,2048]{3,2,1,0:T(8,128)(2,1)}, u32[]{:S(2)}, u32[]{:S(2)}) async-start(bf16[32,1,40,2048]{3,2,1,0:T(8,128)(2,1)} %convert_bitcast_fusion), calls=%async_computation.1 | async-start | bytes 10485760 | tf_op jit(solution)/shard_map/all_to_all | solution.py:140
  265.5 0.0 copy-done.6
  265.5 0.1 copy.57
  266.3 64.9 %all-to-all-done.1 = bf16[32,1,40,2048]{3,2,1,0:T(8,128)(2,1)} async-done(((bf16[32,1,40,2048]{3,2,1,0:T(8,128)(2,1)}), bf16[32,1,40,2048]{3,2,1,0:T(8,128)(2,1)}, u32[]{:S(2)}, u32[]{:S(2)}) %all-to-all-start.1) | async-done | bytes 5242912 | tf_op jit(solution)/shard_map/all_to_all | solution.py:140
  331.1 12.1 %gather_fusion.1 = bf16[1024,2048]{1,0:T(8,128)(2,1)} fusion(bf16[1280,2048]{1,0:T(8,128)(2,1)} %bitcast.34, s32[1024]{0:T(1024)S(1)} %broadcast_clamp_fusion), kind=kCustom, calls=%fused_computation.1 | custom fusion | bytes 8392704 | tf_op jit(solution)/shard_map/gather | solution.py:141
  343.2 6.5 %fusion.12 = f32[128,2048]{1,0:T(8,128)S(1)} fusion(bf16[1024,2048]{1,0:T(8,128)(2,1)} %gather_fusion.1, f32[128,8]{1,0:T(8,128)S(1)} %copy.57), kind=kLoop, calls=%fused_computation.21 | loop fusion | flops 6029312 | bytes 5246976 | tf_op jit(solution)/shard_map/reduce_sum | solution.py:144
  349.7 1.0 fusion.35
  (27 shorter events, 0.2 us)
Async XLA Ops:
  6.5 1.4 copy-start
  6.5 5.5 %copy-start.2 = (bf16[1,1,2,128,2048]{4,3,2,1,0:T(8,128)(2,1)S(1)}, bf16[1,1,2,128,2048]{4,3,2,1,0:T(8,128)(2,1)}, u32[]{:S(2)}) copy-start(bf16[1,1,2,128,2048]{4,3,2,1,0:T(8,128)(2,1)} %param.17) | copy-start | bytes 3145732
  6.5 123.5 %all-gather.2.cloned.1.call-start = ((), (), s32[]{:S(2)}) async-start(), calls=%async_computation.2 | async-start | bytes 15728640 | tf_op jit(solution)/shard_map/all_gather | solution.py:85
  6.5 15.6 %copy-start.4 = (s32[1,1,128,8]{2,3,1,0:T(8,128)S(1)}, s32[1,1,128,8]{2,3,1,0:T(8,128)}, u32[]{:S(2)}) copy-start(s32[1,1,128,8]{2,3,1,0:T(8,128)} %param.24) | copy-start | bytes 12292
  154.2 1.2 copy-start.3
  155.3 4.8 %copy-start.5 = (f32[2048]{0:T(1024)S(1)}, f32[2048]{0:T(1024)}, u32[]{:S(2)}) copy-start(f32[2048]{0:T(1024)} %param.23) | copy-start | bytes 24580
  238.5 13.9 %copy-start.7 = (bf16[1,1024,2048]{2,1,0:T(8,128)(2,1)S(1)}, bf16[1,1024,2048]{2,1,0:T(8,128)(2,1)}, u32[]{:S(2)}) copy-start(bf16[1,1024,2048]{2,1,0:T(8,128)(2,1)} %param.27) | copy-start | bytes 12582916
  260.2 5.2 %copy-start.6 = (f32[1,1,128,8]{2,3,1,0:T(8,128)S(1)}, f32[1,1,128,8]{2,3,1,0:T(8,128)}, u32[]{:S(2)}) copy-start(f32[1,1,128,8]{2,3,1,0:T(8,128)} %param.25) | copy-start | bytes 12292
  260.2 70.9 %all-to-all-start.1 = ((bf16[32,1,40,2048]{3,2,1,0:T(8,128)(2,1)}), bf16[32,1,40,2048]{3,2,1,0:T(8,128)(2,1)}, u32[]{:S(2)}, u32[]{:S(2)}) async-start(bf16[32,1,40,2048]{3,2,1,0:T(8,128)(2,1)} %convert_bitcast_fusion), calls=%async_computation.1 | async-start | bytes 10485760 | tf_op jit(solution)/shard_map/all_to_all | solution.py:140
  331.1 19.6 %copy-start.1 = (s32[1,4]{1,0:T(1,128)S(1)}, s32[1,4]{1,0:T(1,128)}, u32[]{:S(2)}) copy-start(s32[1,4]{1,0:T(1,128)} %param.21) | copy-start | bytes 52
Sparse Core Ops, SparseCore 0:
  9.0 121.0 all-gather.1
where the time goes:
time: 359 us; the launch traced here: 358 us
  waiting for transfers between devices  168 us (47%)
  blocking collectives  69.2 us (19%)
  local copies, waits for them, and re-layouts  45.7 us (13%)
  matrix products  30.3 us (8%)
  other arithmetic  22.3 us (6%)
  between operations  16.2 us (5%)
  starting transfers between devices  5.22 us (1%)
    all_gather x1, waiting for transfers between devices, on_device(): piece = lax.all_gather(prefix_cache, 'req', axis=1, tiled=True)  102 us
    all_to_all x1, blocking collectives, on_device(): lax.all_to_all(outgoing_rows, 'exp', split_axis=0, concat_axis=0, tiled=T...  69.2 us
    all_to_all x1, waiting for transfers between devices, on_device(): lax.all_to_all(produced, 'exp', split_axis=0, concat_axis=0, tiled=True)  64.9 us
    another operation x3, local copies, waits for them, and re-layouts  16.8 us
    dot_general x1, matrix products, on_device(): jnp.einsum('sekd,edf->sekf', lax.all_to_all(outgoing_rows, 'exp', split_a...  13.9 us
    gather x1, local copies, waits for them, and re-layouts, on_device(): returned_rows.reshape(slot_count, width)[slot_of]  12.1 us
    another operation x3, other arithmetic  9.14 us
    dot_general x1, matrix products, on_device(): jnp.einsum('sekf,efd->sekd', hidden_units, expert_downward, preferred_ele...  7.78 us
  transfers between devices with their start and end apart: 2, of which 2 were waited for; matrix products, arithmetic and copies ran while one was open for 5% of the time, Pallas kernels for 0%

commit v1 on v0

--- a/solution.py
+++ b/solution.py
@@ -1,3 +1,4 @@
+import functools
 import jax
 import jax.numpy as jnp
 from jax import lax
@@ -5,6 +6,15 @@
 
 HD = 128
 SINK = 4
+
+
+def proceed_shifts_all_over_axis(view, on_dim):
+    response = jnp.stack(lax.psum(1, "req") * [view])
+    outer = lax.all_to_all(response, "req", 0, 0)
+    return jnp.concatenate(outer, axis=on_dim)
+
+
+values_connect = functools.partial(proceed_shifts_all_over_axis, on_dim=1)
 
 
 def softmax_part(scores, visible, values):
@@ -82,7 +92,7 @@
     blank_stats = jnp.zeros((head_count, row_count), jnp.float32)
     blank_sums = jnp.zeros((head_count, row_count, HD), jnp.float32)
     carry = (blank_stats, blank_stats, blank_sums)
-    piece = lax.all_gather(prefix_cache, "req", axis=1, tiled=True)
+    piece = values_connect(prefix_cache)
     start = jnp.int32(0)
     held = piece.shape[1]
     inside = (owner >= start) & (owner < start + held)

time: 359 us -> 360 us (level)
  waiting for transfers between devices: 168 us -> 185 us
  between operations: 16.2 us -> 2.88 us
  local copies, waits for them, and re-layouts: 45.7 us -> 36.3 us
  starting transfers between devices: 5.22 us -> 11.7 us
    all_to_all x0 -> x1, waiting for transfers between devices: none -> 120 us  [proceed_shifts_all_over_axis(): outer = lax.all_to_all(response, 'req', 0, 0)]
    all_gather x1 -> x0, waiting for transfers between devices: 102 us -> none  [on_device(): piece = lax.all_gather(prefix_cache, 'req', axis=1, tiled=True)]
    another operation x3 -> x4, local copies, waits for them, and re-layouts: 16.8 us -> 9.1 us  [the longest x1 5.58 us: proceed_shifts_all_over_axis(): response = jnp.stack(lax.psum(1, 'req') * [view])]
    all_to_all x0 -> x1, starting transfers between devices: none -> 6.46 us  [proceed_shifts_all_over_axis(): outer = lax.all_to_all(response, 'req', 0, 0)]
where the time goes in v1:
time: 360 us
  waiting for transfers between devices  185 us (51%)
  blocking collectives  70.5 us (20%)
  local copies, waits for them, and re-layouts  36.3 us (10%)
  matrix products  30.3 us (8%)
  other arithmetic  22.3 us (6%)
  starting transfers between devices  11.7 us (3%)
    all_to_all x1, waiting for transfers between devices, proceed_shifts_all_over_axis(): outer = lax.all_to_all(response, 'req', 0, 0)  120 us
    all_to_all x1, blocking collectives, on_device(): lax.all_to_all(outgoing_rows, 'exp', split_axis=0, concat_axis=0, tiled=T...  70.5 us
    all_to_all x1, waiting for transfers between devices, on_device(): lax.all_to_all(produced, 'exp', split_axis=0, concat_axis=0, tiled=True)  64.9 us
    dot_general x1, matrix products, on_device(): jnp.einsum('sekd,edf->sekf', lax.all_to_all(outgoing_rows, 'exp', split_a...  13.9 us
    gather x1, local copies, waits for them, and re-layouts, on_device(): returned_rows.reshape(slot_count, width)[slot_of]  12.1 us
    another operation x3, other arithmetic  9.14 us
    dot_general x1, matrix products, on_device(): jnp.einsum('sekf,efd->sekd', hidden_units, expert_downward, preferred_ele...  7.78 us
  transfers between devices with their start and end apart: 2, of which 2 were waited for; matrix products, arithmetic and copies ran while one was open for 5% of the time, Pallas kernels for 0%

profile of v1, /device:TPU:0, one launch (start us, length us, event | category | flops | bytes accessed | tf_op | source)
XLA Modules:
  0.0 359.8 jit_solution(12396797390207524914)
XLA Ops:
  0.0 3.4 copy.40
  3.4 5.6 %stack.2 = bf16[4,1,1,2,384,2048]{4,5,3,2,1,0:T(8,128)(2,1)} broadcast(bf16[2,384,2048]{1,2,0:T(8,128)(2,1)S(1)} %copy.40), dimensions={3,4,5} | broadcast | bytes 15728640 | tf_op jit(solution)/shard_map/stack | solution.py:12
  9.0 6.5 %all-to-all-start = ((bf16[4,1,1,2,384,2048]{4,5,3,2,1,0:T(8,128)(2,1)}), bf16[4,1,1,2,384,2048]{4,5,3,2,1,0:T(8,128)(2,1)}, u32[]{:S(2)}, u32[]{:S(2)}) async-start(bf16[4,1,1,2,384,2048]{4,5,3,2,1,0:T(8,128)(2,1)} %stack.2), calls=%async_computation | async-start | bytes 25165824 | tf_op jit(solution)/shard_map/all_to_all | solution.py:13
  16.2 0.6 constant_dynamic-slice_fusion.2
  18.0 0.1 copy.50
  18.1 0.1 eq.29
  18.2 0.1 eq.25
  18.3 0.3 copy.41
  18.6 0.0 copy-done.2
  18.6 0.1 fusion.50
  18.7 0.3 copy.66
  19.0 0.3 copy.47
  19.3 9.0 %reduce-window.6 = s32[32,8,128]{2,1,0:T(8,128)S(1)} reduce-window(s32[32,8,128]{2,1,0:T(8,128)S(1)} %fusion.40, s32[]{:T(128)} %constant.26.clone.1), window={size=1x1x128 pad=0_0x0_0x127_0}, to_apply=%region_6.7 | reduce-window | flops 4161536 | bytes 262148 | tf_op jit(solution)/shard_map/reduce-window
  28.3 0.1 slice.38
  28.4 0.1 copy.52
  28.6 0.1 copy.53
  28.7 0.1 copy.49
  28.8 0.1 mul.99
  28.9 0.1 broadcast_add_fusion
  29.1 4.3 %scatter_custom_fusion = s32[1280]{0:T(1024)S(1)} fusion(s32[1024]{0:T(1024)S(1)} %bitcast.118, s32[1024]{0:T(1024)S(1)} %iota.53, s32[]{:T(128)} %constant.59.clone.1), kind=kCustom, calls=%fused_computation.73 | custom fusion | bytes 5124 | tf_op jit(solution)/shard_map/scatter | solution.py:131
  33.4 0.1 broadcast_in_dim.76
  33.6 0.4 fusion.51
  33.9 0.2 fusion.32
  34.1 120.4 %all-to-all-done = bf16[4,1,1,2,384,2048]{4,5,3,2,1,0:T(8,128)(2,1)} async-done(((bf16[4,1,1,2,384,2048]{4,5,3,2,1,0:T(8,128)(2,1)}), bf16[4,1,1,2,384,2048]{4,5,3,2,1,0:T(8,128)(2,1)}, u32[]{:S(2)}, u32[]{:S(2)}) %all-to-all-start) | async-done | bytes 12582944 | tf_op jit(solution)/shard_map/all_to_all | solution.py:13
  154.5 7.5 %conditional.1 = (f32[16,128]{1,0:T(8,128)}, f32[16,128]{1,0:T(8,128)S(1)}, f32[16,128,128]{1,2,0:T(8,128)S(1)}) conditional(s32[]{:T(128)} %convert_element_type.60, () %tuple.13, (s32[]{:T(128)}, bf16[4,1,1,2,384,2048]{4,5,3,2,1,0:T(8,128)(2,1)}, bf16[128,16,128]{0,2,1:T(8,128)(2,1)S(1)}) %tuple.28), branch_computations={%region_0.1_spmd, %region_1.4_spmd} | conditional | flops 411398528 | bytes 20677444 | solution.py:108
  154.5 0.1 fusion.9
  155.2 2.2 constant_dynamic-slice_fusion.1
  157.4 1.4 fusion.2
  158.9 1.7 fusion.3
  160.6 1.4 fusion.1
  161.9 0.0 copy-start.3
  161.9 0.8 multiply_add_fusion
  162.7 0.4 fusion.31
  163.1 0.0 copy-done.3
  163.1 0.0 copy-start.6
  163.1 4.8 %multiply_reduce_fusion = (f32[128]{0:T(128)S(1)}, f32[128,2048]{1,0:T(8,128)S(1)}) fusion(bf16[128,2048]{0,1:T(8,128)(2,1)S(1)} %bitcast.112, bf16[2048,2048]{1,0:T(8,128)(2,1)} %param.22, bf16[1,1,128,2048]{3,2,1,0:T(8,128)(2,1)S(1)} %copy-done.3), kind=kOutput, calls=%fused_computation.42 | convolution fusion | flops 1074790272 | bytes 10486272 | tf_op jit(solution)/shard_map/dot_general | solution.py:111
  167.9 0.2 multiply_convert_fusion
  168.0 6.1 %gather_fusion = bf16[1280,2048]{1,0:T(8,128)(2,1)} fusion(bf16[128,2048]{1,0:T(8,128)(2,1)S(1)} %multiply_convert_fusion, s32[2048]{0:T(1024)S(1)} %pad_clamp_fusion), kind=kCustom, calls=%fused_computation | custom fusion | bytes 10490880 | tf_op jit(solution)/shard_map/gather | solution.py:135
  174.2 2.9 broadcast_select_fusion
  177.1 70.5 %all_to_all.15 = bf16[32,1,40,2048]{3,2,1,0:T(8,128)(2,1)S(1)} all-to-all(bf16[32,1,40,2048]{3,2,1,0:T(8,128)(2,1)S(1)} %broadcast_select_fusion), channel_id=1, replica_groups=mesh['req'=4,'exp'=32] {'exp'}, dimensions={0} | all-to-all | bytes 10485760 | tf_op jit(solution)/shard_map/all_to_all | solution.py:139
  247.6 13.9 %fusion.17 = f32[32,1,40,2048]{3,2,0,1:T(8,128)S(1)} fusion(bf16[1,2048,2048]{2,1,0:T(8,128)(2,1)} %param.26, bf16[32,1,40,2048]{3,2,1,0:T(8,128)(2,1)S(1)} %all_to_all.15), kind=kOutput, calls=%fused_computation.29 | convolution fusion | flops 10737418240 | bytes 24117248 | tf_op jit(solution)/shard_map/sekd,edf->sekf/dot_general | solution.py:137
  261.5 7.8 %convert_bitcast_fusion = bf16[32,1,40,2048]{3,2,1,0:T(8,128)(2,1)} fusion(bf16[1,1024,2048]{2,1,0:T(8,128)(2,1)S(1)} %copy-done.8, f32[32,1,40,2048]{3,2,0,1:T(8,128)S(1)} %fusion.17), kind=kOutput, calls=%fused_computation.27 | convolution fusion | flops 5379194880 | bytes 19922944 | tf_op jit(solution)/shard_map/sekf,efd->sekd/dot_general | solution.py:147
  269.3 5.2 %all-to-all-start.2 = ((bf16[32,1,40,2048]{3,2,1,0:T(8,128)(2,1)}), bf16[32,1,40,2048]{3,2,1,0:T(8,128)(2,1)}, u32[]{:S(2)}, u32[]{:S(2)}) async-start(bf16[32,1,40,2048]{3,2,1,0:T(8,128)(2,1)} %convert_bitcast_fusion), calls=%async_computation.2 | async-start | bytes 10485760 | tf_op jit(solution)/shard_map/all_to_all | solution.py:150
  274.5 0.1 copy.56
  275.3 64.9 %all-to-all-done.2 = bf16[32,1,40,2048]{3,2,1,0:T(8,128)(2,1)} async-done(((bf16[32,1,40,2048]{3,2,1,0:T(8,128)(2,1)}), bf16[32,1,40,2048]{3,2,1,0:T(8,128)(2,1)}, u32[]{:S(2)}, u32[]{:S(2)}) %all-to-all-start.2) | async-done | bytes 5242912 | tf_op jit(solution)/shard_map/all_to_all | solution.py:150
  340.1 12.1 %gather_fusion.1 = bf16[1024,2048]{1,0:T(8,128)(2,1)} fusion(bf16[1280,2048]{1,0:T(8,128)(2,1)} %bitcast.34, s32[1024]{0:T(1024)S(1)} %broadcast_clamp_fusion), kind=kCustom, calls=%fused_computation.1 | custom fusion | bytes 8392704 | tf_op jit(solution)/shard_map/gather | solution.py:151
  352.2 6.5 %fusion.12 = f32[128,2048]{1,0:T(8,128)S(1)} fusion(bf16[1024,2048]{1,0:T(8,128)(2,1)} %gather_fusion.1, f32[128,8]{1,0:T(8,128)S(1)} %copy.56), kind=kLoop, calls=%fused_computation.21 | loop fusion | flops 6029312 | bytes 5246976 | tf_op jit(solution)/shard_map/reduce_sum | solution.py:154
  358.7 1.0 fusion.35
  (29 shorter events, 0.2 us)
Async XLA Ops:
  0.0 16.2 %copy-start = (s32[1,4]{1,0:T(1,128)S(1)}, s32[1,4]{1,0:T(1,128)}, u32[]{:S(2)}) copy-start(s32[1,4]{1,0:T(1,128)} %param.21) | copy-start | bytes 52
  9.0 9.0 %copy-start.5 = (s32[1,1,128,8]{2,3,1,0:T(8,128)S(1)}, s32[1,1,128,8]{2,3,1,0:T(8,128)}, u32[]{:S(2)}) copy-start(s32[1,1,128,8]{2,3,1,0:T(8,128)} %param.24) | copy-start | bytes 12292
  9.0 9.3 %copy-start.4 = (bf16[1,1,128,2048]{3,2,1,0:T(8,128)(2,1)S(1)}, bf16[1,1,128,2048]{3,2,1,0:T(8,128)(2,1)}, u32[]{:S(2)}) copy-start(bf16[1,1,128,2048]{3,2,1,0:T(8,128)(2,1)} %param.16) | copy-start | bytes 1572868
  9.0 9.6 %copy-start.2 = (bf16[1,1,2,128,2048]{4,3,2,1,0:T(8,128)(2,1)S(1)}, bf16[1,1,2,128,2048]{4,3,2,1,0:T(8,128)(2,1)}, u32[]{:S(2)}) copy-start(bf16[1,1,2,128,2048]{4,3,2,1,0:T(8,128)(2,1)} %param.17) | copy-start | bytes 3145732
  9.0 145.4 %all-to-all-start = ((bf16[4,1,1,2,384,2048]{4,5,3,2,1,0:T(8,128)(2,1)}), bf16[4,1,1,2,384,2048]{4,5,3,2,1,0:T(8,128)(2,1)}, u32[]{:S(2)}, u32[]{:S(2)}) async-start(bf16[4,1,1,2,384,2048]{4,5,3,2,1,0:T(8,128)(2,1)} %stack.2), calls=%async_computation | async-start | bytes 25165824 | tf_op jit(solution)/shard_map/all_to_all | solution.py:13
  161.9 1.2 copy-start.3
  163.1 4.8 %copy-start.6 = (f32[2048]{0:T(1024)S(1)}, f32[2048]{0:T(1024)}, u32[]{:S(2)}) copy-start(f32[2048]{0:T(1024)} %param.23) | copy-start | bytes 24580
  247.5 13.9 %copy-start.8 = (bf16[1,1024,2048]{2,1,0:T(8,128)(2,1)S(1)}, bf16[1,1024,2048]{2,1,0:T(8,128)(2,1)}, u32[]{:S(2)}) copy-start(bf16[1,1024,2048]{2,1,0:T(8,128)(2,1)} %param.27) | copy-start | bytes 12582916
  269.2 5.2 %copy-start.7 = (f32[1,1,128,8]{2,3,1,0:T(8,128)S(1)}, f32[1,1,128,8]{2,3,1,0:T(8,128)}, u32[]{:S(2)}) copy-start(f32[1,1,128,8]{2,3,1,0:T(8,128)} %param.25) | copy-start | bytes 12292
  269.3 70.9 %all-to-all-start.2 = ((bf16[32,1,40,2048]{3,2,1,0:T(8,128)(2,1)}), bf16[32,1,40,2048]{3,2,1,0:T(8,128)(2,1)}, u32[]{:S(2)}, u32[]{:S(2)}) async-start(bf16[32,1,40,2048]{3,2,1,0:T(8,128)(2,1)} %convert_bitcast_fusion), calls=%async_computation.2 | async-start | bytes 10485760 | tf_op jit(solution)/shard_map/all_to_all | solution.py:150
  340.1 19.6 %copy-start.1 = (s32[1,4]{1,0:T(1,128)S(1)}, s32[1,4]{1,0:T(1,128)}, u32[]{:S(2)}) copy-start(s32[1,4]{1,0:T(1,128)} %param.21) | copy-start | bytes 52
